TPU v7x, 128 devices: a whole 4x4x4 slice. The times are simulated.
128 devices in a mesh: dp: 16 (over x, y), expert: 8 (over z, core).
Axes of the slice: x: 4, y: 4, z: 4, core: 2. Of those that a mesh axis runs over, the one named last changes fastest.
Arguments:
- tokens: bfloat16 [2048, 4096], P('dp', 'expert'), may hold values from -6 to 6
- output_gradient: bfloat16 [2048, 4096], P('dp', 'expert'), may hold values from -6 to 6
- routing: int32 [2048, 2], P('dp'), may hold values from 0 to 7, all different within a row; in each aligned block of 128 rows (0 to 127, 128 to 255, ...) at most 96 rows name the same one
- router_gate_values: float32 [2048, 2], P('dp'), may hold values from 0.1 to 0.9
- gate_weight: bfloat16 [8, 7168, 4096], P('expert', 'dp'), may hold values from -0.09375 to 0.09375
- up_weight: bfloat16 [8, 7168, 4096], P('expert', 'dp'), may hold values from -0.09375 to 0.09375
- down_weight: bfloat16 [8, 7168, 4096], P('expert', 'dp'), may hold values from -0.0625 to 0.0625
- adapter_lower_gate: bfloat16 [8, 16, 4096], P('expert'), may hold values from -0.09375 to 0.09375
- adapter_upper_gate: bfloat16 [8, 7168, 16], P('expert', 'dp'), may hold values from -0.375 to 0.375
- adapter_lower_up: bfloat16 [8, 16, 4096], P('expert'), may hold values from -0.09375 to 0.09375
- adapter_upper_up: bfloat16 [8, 7168, 16], P('expert', 'dp'), may hold values from -0.375 to 0.375
- adapter_lower_down: bfloat16 [8, 16, 7168], P('expert', None, 'dp'), may hold values from -0.0625 to 0.0625
- adapter_upper_down: bfloat16 [8, 4096, 16], P('expert'), may hold values from -0.375 to 0.375
Outputs:
- grad_x: bfloat16 [2048, 4096], P('dp', 'expert')
- grad_lora_a_gate: float32 [8, 16, 4096], P('expert')
- grad_lora_b_gate: float32 [8, 7168, 16], P('expert', 'dp')
- grad_lora_a_up: float32 [8, 16, 4096], P('expert')
- grad_lora_b_up: float32 [8, 7168, 16], P('expert', 'dp')
- grad_lora_a_down: float32 [8, 16, 7168], P('expert', None, 'dp')
- grad_lora_b_down: float32 [8, 4096, 16], P('expert')
Inputs may be any that keep to these rules, and one draw needn't show every extreme that they name: `routing`: each row names two different experts. In the rows of one dp shard (aligned blocks of 128 rows) no expert is named by more than 96 rows, and in some blocks one expert is named by exactly 96 rows.
All inputs are finite; a program needn't handle non-finite values.
Results may differ from a plain program's by a relative error of at most 0.015.
Values may be sent and summed in bfloat16 or wider, within the bound.
A program may use at most 256 MiB of HBM per device.

v0:
```python
import jax
import jax.numpy as jnp
from jax import lax
from jax.sharding import PartitionSpec as P

ADAPTER_SCALE = 2.0
NUM_CHUNKS = 2


def contract_pair(left, right, left_axis, right_axis):
    return lax.dot_general(
        left, right, (((left_axis,), (right_axis,)), ((), ())), preferred_element_type=jnp.float32
    )


def slot_numbers(route_rows, experts):
    picked = (route_rows[:, :, None] == jnp.arange(experts, dtype=jnp.int32)[None, None, :]).astype(
        jnp.int32
    )
    per_token = jnp.sum(picked, axis=1)
    earlier = jnp.cumsum(per_token, axis=0) - per_token
    return jnp.sum(earlier[:, None, :] * picked, axis=2)


def slot_sources(route_rows, positions, experts, capacity):
    tokens_here, choose = route_rows.shape
    target = (route_rows * capacity + positions).reshape(-1)
    owners = jnp.repeat(jnp.arange(tokens_here, dtype=jnp.int32), choose)
    member_ids = jnp.tile(jnp.arange(choose, dtype=jnp.int32), tokens_here)
    source = jnp.full((experts * capacity,), tokens_here, jnp.int32).at[target].set(owners)
    member = jnp.zeros((experts * capacity,), jnp.int32).at[target].set(member_ids)
    return (source, member)


def rows_backward_pass(input_rows, output_gradient_rows, params):
    (
        gate_weight,
        up_weight,
        down_weight,
        a_gate,
        gate_adapter_upper,
        a_up,
        up_adapter_upper,
        down_adapter_lower,
        b_down,
    ) = params
    gate_projected_lower = contract_pair(a_gate, input_rows, 1, 1).astype(jnp.bfloat16)
    up_projected_lower = contract_pair(a_up, input_rows, 1, 1).astype(jnp.bfloat16)
    gate_preactivation = contract_pair(
        gate_weight, input_rows, 1, 1
    ) + ADAPTER_SCALE * contract_pair(gate_adapter_upper, gate_projected_lower, 1, 0)
    up_preactivation = contract_pair(up_weight, input_rows, 1, 1) + ADAPTER_SCALE * contract_pair(
        up_adapter_upper, up_projected_lower, 1, 0
    )
    sigmoid_gate = jax.nn.sigmoid(gate_preactivation)
    silu_gate = gate_preactivation * sigmoid_gate
    hidden_units = (silu_gate * up_preactivation).astype(jnp.bfloat16)
    down_projected_lower = contract_pair(b_down, output_gradient_rows, 0, 1).astype(jnp.bfloat16)
    hidden_gradient = contract_pair(
        down_weight, output_gradient_rows, 1, 1
    ) + ADAPTER_SCALE * contract_pair(down_adapter_lower, down_projected_lower, 0, 0)
    gate_gradient = (
        hidden_gradient
        * up_preactivation
        * sigmoid_gate
        * (1.0 + gate_preactivation * (1.0 - sigmoid_gate))
    ).astype(jnp.bfloat16)
    up_gradient = (hidden_gradient * silu_gate).astype(jnp.bfloat16)
    gate_partial = contract_pair(gate_adapter_upper, gate_gradient, 0, 0).astype(jnp.bfloat16)
    up_partial = contract_pair(up_adapter_upper, up_gradient, 0, 0).astype(jnp.bfloat16)
    down_partial = contract_pair(down_adapter_lower, hidden_units, 1, 0).astype(jnp.bfloat16)
    paired_partials = jnp.concatenate([gate_partial, up_partial], 0)
    paired_factors = jnp.concatenate([a_gate, a_up], 0)
    gradient_rows_out = (
        contract_pair(gate_gradient, gate_weight, 0, 0)
        + contract_pair(up_gradient, up_weight, 0, 0)
        + ADAPTER_SCALE * contract_pair(paired_partials, paired_factors, 0, 0)
    )
    shared_slice = (
        ADAPTER_SCALE * contract_pair(gate_partial, input_rows, 1, 0),
        ADAPTER_SCALE * contract_pair(up_partial, input_rows, 1, 0),
        ADAPTER_SCALE * contract_pair(output_gradient_rows, down_partial, 0, 1),
    )
    owned_slice = (
        ADAPTER_SCALE * contract_pair(gate_gradient, gate_projected_lower, 1, 1),
        ADAPTER_SCALE * contract_pair(up_gradient, up_projected_lower, 1, 1),
        ADAPTER_SCALE * contract_pair(down_projected_lower, hidden_units, 1, 1),
    )
    return (gradient_rows_out, shared_slice, owned_slice)


def local(
    tokens,
    output_gradient,
    routing,
    router_gate_values,
    gate_weight,
    up_weight,
    down_weight,
    adapter_lower_gate,
    adapter_upper_gate,
    adapter_lower_up,
    adapter_upper_up,
    adapter_lower_down,
    adapter_upper_down,
):
    experts = lax.axis_size("expert")
    shards = lax.axis_size("dp")
    tok_local, feat_local = tokens.shape
    choose = routing.shape[1]
    complete_width = feat_local * experts
    capacity = min(tok_local, 6 * tok_local // experts)
    adapter_rank = adapter_lower_gate.shape[1]
    chunks = NUM_CHUNKS
    piece = capacity // chunks
    params = (
        gate_weight[0],
        up_weight[0],
        down_weight[0],
        adapter_lower_gate[0],
        adapter_upper_gate[0],
        adapter_lower_up[0],
        adapter_upper_up[0],
        adapter_lower_down[0],
        adapter_upper_down[0],
    )
    positions = slot_numbers(routing, experts)
    zero_row = jnp.zeros((1, feat_local), jnp.bfloat16)
    source, member = slot_sources(routing, positions, experts, capacity)
    clamped = jnp.minimum(source, tok_local - 1)
    slot_gate = jnp.where(
        source < tok_local, router_gate_values.reshape(-1)[clamped * choose + member], 0.0
    )
    send_x = jnp.concatenate([tokens, zero_row], 0)[source].reshape(experts, capacity, feat_local)
    send_dy = (
        (
            slot_gate[:, None]
            * jnp.concatenate([output_gradient, zero_row], 0)[source].astype(jnp.float32)
        )
        .astype(jnp.bfloat16)
        .reshape(experts, capacity, feat_local)
    )
    send_both = jnp.concatenate([send_x, send_dy], axis=2)
    recv_both = lax.all_to_all(send_both, "expert", split_axis=0, concat_axis=2, tiled=True)[0]
    recv_both = recv_both.reshape(capacity, experts, 2, feat_local).transpose(0, 2, 1, 3)
    recv_both = recv_both.reshape(capacity, 2 * complete_width)
    rows_pieces = []
    shared_total = None
    owned_total = None
    for c in range(chunks):
        part = recv_both[c * piece : (c + 1) * piece]
        gathered = lax.all_gather(part, "dp", axis=0, tiled=True)
        x_rows = gathered[:, :complete_width]
        dy_rows = gathered[:, complete_width:]
        rows_out, shared_slice, owned_slice = rows_backward_pass(x_rows, dy_rows, params)
        if c == 0:
            shared_total, owned_total = (shared_slice, owned_slice)
        else:
            shared_total = jax.tree.map(jnp.add, shared_total, shared_slice)
            owned_total = jax.tree.map(jnp.add, owned_total, owned_slice)
        rows_bf = rows_out.astype(jnp.bfloat16).reshape(shards, piece, complete_width)
        summed = lax.psum_scatter(rows_bf, "dp", scatter_dimension=0, tiled=True)[0]
        rows_pieces.append(summed)
    lora = jnp.concatenate([shared_total[0], shared_total[1], shared_total[2].T], 0).astype(
        jnp.bfloat16
    )
    lora_shape = lora.shape
    lora_part = lax.psum_scatter(
        lora.reshape(shards * 8, -1), "dp", scatter_dimension=0, tiled=True
    )
    summed = jnp.concatenate(rows_pieces, 0)
    lora_part = lax.optimization_barrier(lora_part)
    lora_sum = lax.all_gather(lora_part, "dp", axis=0, tiled=True).astype(jnp.float32)
    lora_sum = lora_sum.reshape(lora_shape)
    grad_a_gate = lora_sum[:adapter_rank]
    grad_a_up = lora_sum[adapter_rank : 2 * adapter_rank]
    grad_b_down = lora_sum[2 * adapter_rank :].T
    returned_rows = lax.all_to_all(
        summed.reshape(capacity, experts, feat_local),
        "expert",
        split_axis=1,
        concat_axis=1,
        tiled=True,
    ).astype(jnp.float32)
    lookup = positions * experts + routing
    grad_x = jnp.sum(returned_rows.reshape(capacity * experts, feat_local)[lookup], axis=1).astype(
        jnp.bfloat16
    )
    return (
        grad_x,
        grad_a_gate[None],
        owned_total[0][None],
        grad_a_up[None],
        owned_total[1][None],
        owned_total[2][None],
        grad_b_down[None],
    )


def solution(mesh):
    return jax.shard_map(
        local,
        mesh=mesh,
        in_specs=(
            P("dp", "expert"),
            P("dp", "expert"),
            P("dp", None),
            P("dp", None),
            P("expert", "dp", None),
            P("expert", "dp", None),
            P("expert", "dp", None),
            P("expert", None, None),
            P("expert", "dp", None),
            P("expert", None, None),
            P("expert", "dp", None),
            P("expert", None, "dp"),
            P("expert", None, None),
        ),
        out_specs=(
            P("dp", "expert"),
            P("expert", None, None),
            P("expert", "dp", None),
            P("expert", None, None),
            P("expert", "dp", None),
            P("expert", None, "dp"),
            P("expert", None, None),
        ),
        check_vma=False,
    )
```

profile of v0, /device:TPU:1, one launch (start us, length us, event | category | flops | bytes accessed | tf_op | source)
XLA Modules:
  0.0 568.4 jit_solution(9020184322485059997)
XLA Ops:
  7.2 0.8 convert_reduce_fusion
  8.4 0.7 select_reduce_fusion
  9.1 1.3 compare_select_fusion.3
  10.9 0.8 copy.56
  11.8 1.4 scatter_custom_fusion.1
  13.3 1.4 scatter_custom_fusion
  14.7 5.0 gather_fusion.1
  19.8 2.7 gather_fusion.2
  22.5 2.7 gather_fusion
  25.7 27.4 %all_to_all.20 = bf16[8,96,1024]{2,1,0:T(8,128)(2,1)S(1)} all-to-all(bf16[8,96,1024]{2,1,0:T(8,128)(2,1)S(1)} %pad_maximum_fusion), channel_id=1, replica_groups=mesh['dp'=16,'expert'=8] {'expert'}, dimensions={0} | all-to-all | bytes 3145728 | tf_op jit(solution)/shard_map/all_to_all | solution.py:144
  53.0 1.2 reshape.172
  54.2 1.7 copy.71
  56.0 1.3 fusion.132
  57.5 1.3 copy.65
  59.0 1.3 copy.67
  60.7 88.0 %all-gather.3.cloned.1.call-done = bf16[768,8192]{1,0:T(8,128)(2,1)} async-done(((bf16[48,8192]{1,0:T(8,128)(2,1)}), bf16[768,8192]{1,0:T(8,128)(2,1)}) %all-gather.3.cloned.1.call-update) | async-done | bytes 12582928 | tf_op jit(solution)/shard_map/all_gather | solution.py:152
  148.7 4.7 fusion.79
  153.4 6.0 %fusion.31 = f32[768,448]{0,1:T(8,128)S(1)} fusion(bf16[1,448,4096]{2,1,0:T(8,128)(2,1)S(1)} %copy-done.2, bf16[768,8192]{1,0:T(8,128)(2,1)} %all-gather.3.cloned.1.call-done), kind=kOutput, calls=%fused_computation.35 | convolution fusion | flops 2818572288 | bytes 11337728 | tf_op jit(solution)/shard_map/dot_general | solution.py:11
  159.9 1.7 fusion.88
  161.6 0.7 copy-done.34
  162.3 3.1 fusion.10
  165.8 1.7 fusion.76
  167.9 14.7 %fusion.39 = f32[768,448]{0,1:T(8,128)S(1)} fusion(bf16[1,448,4096]{2,1,0:T(8,128)(2,1)S(1)} %copy-done.4, bf16[768,8192]{1,0:T(8,128)(2,1)S(1)} %bitcast.166), kind=kOutput, calls=%fused_computation.43 | convolution fusion | flops 2818572288 | bytes 11337728 | tf_op jit(solution)/shard_map/dot_general | solution.py:11
  182.6 1.8 multiply_convert_fusion.1
  184.8 6.6 %fusion.29 = f32[768,4096]{1,0:T(8,128)} fusion(bf16[448,768]{1,0:T(8,128)(2,1)S(1)} %get-tuple-element.8, bf16[1,448,4096]{2,1,0:T(8,128)(2,1)S(1)} %copy-done.2), kind=kOutput, calls=%fused_computation.33 | convolution fusion | flops 2818572288 | bytes 16941056 | tf_op jit(solution)/shard_map/dot_general | solution.py:11
  191.4 6.5 %fusion.37 = f32[768,4096]{1,0:T(8,128)} fusion(bf16[448,768]{1,0:T(8,128)(2,1)S(1)} %get-tuple-element.9, bf16[1,448,4096]{2,1,0:T(8,128)(2,1)S(1)} %copy-done.4), kind=kOutput, calls=%fused_computation.41 | convolution fusion | flops 2818572288 | bytes 16941056 | tf_op jit(solution)/shard_map/dot_general | solution.py:11
  197.9 42.7 %all-gather.5.cloned.1.call-done = bf16[768,8192]{1,0:T(8,128)(2,1)} async-done(((bf16[48,8192]{1,0:T(8,128)(2,1)}), bf16[768,8192]{1,0:T(8,128)(2,1)}) %all-gather.5.cloned.1.call-update) | async-done | bytes 12582928 | tf_op jit(solution)/shard_map/all_gather | solution.py:152
  240.5 4.7 fusion.91
  245.2 6.0 %fusion.4 = f32[768,448]{0,1:T(8,128)S(1)} fusion(bf16[768,8192]{1,0:T(8,128)(2,1)} %all-gather.5.cloned.1.call-done, bf16[1,448,4096]{2,1,0:T(8,128)(2,1)S(1)} %copy-done.35), kind=kOutput, calls=%fused_computation.12 | convolution fusion | flops 2818572288 | bytes 11337728 | tf_op jit(solution)/shard_map/dot_general | solution.py:11
  251.7 1.7 fusion.85
  253.7 3.1 fusion.27
  257.2 1.7 fusion.82
  259.2 3.3 fusion.35
  262.5 1.8 multiply_convert_fusion
  265.0 1.6 fusion.53
  266.6 0.9 fusion.51
  267.6 4.1 fusion
  271.7 4.4 fusion.23
  276.0 4.4 fusion.24
  280.4 4.1 fusion.20
  284.5 1.0 pad_maximum_fusion.2
  285.5 1.2 convert_element_type.133
  286.9 12.2 %add_convert_fusion.1 = bf16[768,4096]{1,0:T(8,128)(2,1)} fusion(f32[768,4096]{1,0:T(8,128)} %fusion.29, f32[768,4096]{1,0:T(8,128)} %fusion.37, bf16[16,4096]{1,0:T(8,128)(2,1)S(1)} %bitcast.186, bf16[16,4096]{1,0:T(8,128)(2,1)S(1)} %bitcast.184, bf16[16,768]{1,0:T(8,128)(2,1)} %bitcast.191, bf16[16,768]{1,0:T(8,128)(2,1)} %bitcast.190), kind=kOutput, calls=%fused_computation.7 | convolution fusion | flops 214532096 | bytes 31768576 | tf_op jit(solution)/shard_map/dot_general | solution.py:11
  299.2 8.9 %fusion.25 = f32[768,4096]{1,0:T(8,128)} fusion(bf16[448,768]{1,0:T(8,128)(2,1)S(1)} %get-tuple-element.11, bf16[1,448,4096]{2,1,0:T(8,128)(2,1)} %param.17), kind=kOutput, calls=%fused_computation.29 | convolution fusion | flops 2818572288 | bytes 16941056 | tf_op jit(solution)/shard_map/dot_general | solution.py:11
  308.1 6.4 %fusion.33 = f32[768,4096]{1,0:T(8,128)} fusion(bf16[448,768]{1,0:T(8,128)(2,1)S(1)} %get-tuple-element.12, bf16[1,448,4096]{2,1,0:T(8,128)(2,1)S(1)} %copy-done.6), kind=kOutput, calls=%fused_computation.37 | convolution fusion | flops 2818572288 | bytes 16941056 | tf_op jit(solution)/shard_map/dot_general | solution.py:11
  314.5 12.1 %add_convert_fusion = bf16[768,4096]{1,0:T(8,128)(2,1)} fusion(f32[768,4096]{1,0:T(8,128)} %fusion.25, f32[768,4096]{1,0:T(8,128)} %fusion.33, bf16[16,4096]{1,0:T(8,128)(2,1)S(1)} %bitcast.187, bf16[16,4096]{1,0:T(8,128)(2,1)S(1)} %bitcast.185, bf16[16,768]{1,0:T(8,128)(2,1)S(1)} %bitcast.193, bf16[16,768]{1,0:T(8,128)(2,1)S(1)} %bitcast.192), kind=kOutput, calls=%fused_computation.6 | convolution fusion | flops 214532096 | bytes 31768576 | tf_op jit(solution)/shard_map/dot_general | solution.py:11
  327.6 0.6 dynamic-slice
  328.8 1.4 fusion.135
  330.2 2.1 fusion.95
  332.6 1.0 fusion.97
  333.8 1.0 fusion.99
  334.8 34.6 %all-reduce.7.cloned.1.call-done = bf16[128,1536]{1,0:T(8,128)(2,1)} async-done(((bf16[128,1536]{1,0:T(8,128)(2,1)}), bf16[128,1536]{1,0:T(8,128)(2,1)}) %all-reduce.7.cloned.1.call-update) | async-done | bytes 393232
  369.4 0.7 constant_dynamic-slice_fusion
  370.1 18.3 %all_gather.11 = bf16[128,1536]{1,0:T(8,128)(2,1)S(1)} all-gather(bf16[8,1536]{1,0:T(8,128)(2,1)S(1)} %constant_dynamic-slice_fusion), channel_id=1, replica_groups=mesh['dp'=16,'expert'=8] {'dp'}, dimensions={0}, use_global_device_ids=true | all-gather | bytes 417792 | tf_op jit(solution)/shard_map/all_gather | solution.py:173
  388.9 65.0 %reduce-scatter.7.cloned.1.call-done = bf16[1,48,4096]{2,1,0:T(8,128)(2,1)} async-done(((bf16[16,48,4096]{2,1,0:T(8,128)(2,1)}), bf16[1,48,4096]{2,1,0:T(8,128)(2,1)}) %reduce-scatter.7.cloned.1.call-update) | async-done | bytes 393232
  453.9 1.1 copy.66
  455.1 82.5 %reduce-scatter.9.cloned.1.call-done = bf16[1,48,4096]{2,1,0:T(8,128)(2,1)} async-done(((bf16[16,48,4096]{2,1,0:T(8,128)(2,1)}), bf16[1,48,4096]{2,1,0:T(8,128)(2,1)}) %reduce-scatter.9.cloned.1.call-update) | async-done | bytes 393232
  537.7 1.1 copy.68
  538.9 1.0 pad_maximum_fusion.1
  539.9 6.2 %all-to-all-start.1 = ((bf16[96,8,512]{2,0,1:T(8,128)(2,1)}), bf16[96,8,512]{2,0,1:T(8,128)(2,1)S(1)}, u32[]{:S(2)}, u32[]{:S(2)}) async-start(bf16[96,8,512]{2,0,1:T(8,128)(2,1)} %pad_maximum_fusion.1), calls=%async_computation.1 | async-start | bytes 1572864 | tf_op jit(solution)/shard_map/all_to_all | solution.py:178
  546.1 0.9 slice_bitcast_fusion
  547.0 11.4 %all-to-all-done.1 = bf16[96,8,512]{2,0,1:T(8,128)(2,1)S(1)} async-done(((bf16[96,8,512]{2,0,1:T(8,128)(2,1)}), bf16[96,8,512]{2,0,1:T(8,128)(2,1)S(1)}, u32[]{:S(2)}, u32[]{:S(2)}) %all-to-all-start.1) | async-done | bytes 786464 | tf_op jit(solution)/shard_map/all_to_all | solution.py:178
  558.8 1.0 gather_fusion.3
  560.1 1.3 reduce_sum.29
  (144 shorter events, 9.0 us)
Async XLA Ops:
  7.2 152.7 %copy-start = (bf16[1,4096,16]{1,2,0:T(8,128)(2,1)S(1)}, bf16[1,4096,16]{1,2,0:T(8,128)(2,1)}, u32[]{:S(2)}) copy-start(bf16[1,4096,16]{1,2,0:T(8,128)(2,1)} %param.25) | copy-start | bytes 393220
  7.2 12.6 %copy-start.18 = (bf16[128,512]{1,0:T(8,128)(2,1)S(1)}, bf16[128,512]{1,0:T(8,128)(2,1)}, u32[]{:S(2)}) copy-start(bf16[128,512]{1,0:T(8,128)(2,1)} %param.14) | copy-start | bytes 393220
  7.2 12.6 %copy-start.19 = (bf16[128,512]{1,0:T(8,128)(2,1)S(1)}, bf16[128,512]{1,0:T(8,128)(2,1)}, u32[]{:S(2)}) copy-start(bf16[128,512]{1,0:T(8,128)(2,1)} %param.13) | copy-start | bytes 393220
  7.2 141.5 %all-gather.3.cloned.1.call-start = ((), (), s32[]{:S(2)}) async-start(), calls=%async_computation.4 | async-start | bytes 13369344 | tf_op jit(solution)/shard_map/all_gather | solution.py:152
  57.3 91.4 %copy-start.7 = (bf16[1,16,4096]{2,1,0:T(8,128)(2,1)S(1)}, bf16[1,16,4096]{2,1,0:T(8,128)(2,1)}, u32[]{:S(2)}) copy-start(bf16[1,16,4096]{2,1,0:T(8,128)(2,1)} %param.20) | copy-start | bytes 393220
  58.8 181.7 %all-gather.5.cloned.1.call-start = ((), (), s32[]{:S(2)}) async-start(), calls=%async_computation.5 | async-start | bytes 13369344 | tf_op jit(solution)/shard_map/all_gather | solution.py:152
  60.4 309.0 %all-reduce.7.cloned.1.call-start = ((), (), s32[]{:S(2)}) async-start(), calls=%async_computation.6 | async-start | bytes 786432
  148.7 4.7 copy-start.2
  148.7 11.1 %slice-start = ((s8[12582912]{0:T(1024)(128)(4,1)}), s8[4194304]{0:T(1024)(128)(4,1)S(1)}, s32[]{:S(2)}) async-start(s8[12582912]{0:T(1024)(128)(4,1)} %bitcast.165), calls=%async_computation.9 | async-start | bytes 8388608
  153.4 6.0 %copy-start.20 = (bf16[768,16]{0,1:T(8,128)(2,1)}, bf16[768,16]{0,1:T(8,128)(2,1)S(1)}, u32[]{:S(2)}) copy-start(bf16[768,16]{0,1:T(8,128)(2,1)S(1)} %fusion.79) | copy-start | bytes 73732
  153.4 6.0 %copy-start.11 = (bf16[1,448,16]{1,2,0:T(8,128)(2,1)S(1)}, bf16[1,448,16]{1,2,0:T(8,128)(2,1)}, u32[]{:S(2)}) copy-start(bf16[1,448,16]{1,2,0:T(8,128)(2,1)} %param.21) | copy-start | bytes 43012
  153.4 6.4 %slice-start.1 = ((s8[12582912]{0:T(1024)(128)(4,1)}), s8[4194304]{0:T(1024)(128)(4,1)S(1)}, s32[]{:S(2)}) async-start(s8[12582912]{0:T(1024)(128)(4,1)} %bitcast.165), calls=%async_computation.10 | async-start | bytes 8388608
  153.4 6.4 %slice-start.2 = ((s8[12582912]{0:T(1024)(128)(4,1)}), s8[4194304]{0:T(1024)(128)(4,1)S(1)}, s32[]{:S(2)}) async-start(s8[12582912]{0:T(1024)(128)(4,1)} %bitcast.165), calls=%async_computation.11 | async-start | bytes 8388608
  159.9 2.4 copy-start.34
  162.3 3.1 copy-start.22
  162.3 3.1 copy-start.10
  162.3 3.5 copy-start.8
  165.8 2.1 copy-start.4
  167.9 14.7 %copy-start.29 = (bf16[768,16]{0,1:T(8,128)(2,1)}, bf16[768,16]{0,1:T(8,128)(2,1)S(1)}, u32[]{:S(2)}) copy-start(bf16[768,16]{0,1:T(8,128)(2,1)S(1)} %fusion.76) | copy-start | bytes 73732
  167.9 14.7 %copy-start.28 = (bf16[1,448,16]{1,2,0:T(8,128)(2,1)S(1)}, bf16[1,448,16]{1,2,0:T(8,128)(2,1)}, u32[]{:S(2)}) copy-start(bf16[1,448,16]{1,2,0:T(8,128)(2,1)} %param.23) | copy-start | bytes 43012
  184.6 80.2 %copy-start.12 = (bf16[768,16]{0,1:T(8,128)(2,1)}, bf16[768,16]{0,1:T(8,128)(2,1)S(1)}, u32[]{:S(2)}) copy-start(bf16[768,16]{0,1:T(8,128)(2,1)S(1)} %convolution_convert_fusion.5) | copy-start | bytes 73732
  184.8 81.9 %copy-start.13 = (bf16[768,16]{0,1:T(8,128)(2,1)}, bf16[768,16]{0,1:T(8,128)(2,1)S(1)}, u32[]{:S(2)}) copy-start(bf16[768,16]{0,1:T(8,128)(2,1)S(1)} %convolution_convert_fusion.4) | copy-start | bytes 73732
  240.5 4.7 copy-start.35
  240.5 11.1 %slice-start.6 = ((s8[12582912]{0:T(1024)(128)(4,1)}), s8[4194304]{0:T(1024)(128)(4,1)S(1)}, s32[]{:S(2)}) async-start(s8[12582912]{0:T(1024)(128)(4,1)} %bitcast.169), calls=%async_computation.15 | async-start | bytes 8388608
  245.2 6.0 %copy-start.26 = (bf16[768,16]{0,1:T(8,128)(2,1)}, bf16[768,16]{0,1:T(8,128)(2,1)S(1)}, u32[]{:S(2)}) copy-start(bf16[768,16]{0,1:T(8,128)(2,1)S(1)} %fusion.91) | copy-start | bytes 73732
  245.2 6.4 %slice-start.7 = ((s8[12582912]{0:T(1024)(128)(4,1)}), s8[4194304]{0:T(1024)(128)(4,1)S(1)}, s32[]{:S(2)}) async-start(s8[12582912]{0:T(1024)(128)(4,1)} %bitcast.169), calls=%async_computation.16 | async-start | bytes 8388608
  245.2 6.4 %slice-start.8 = ((s8[12582912]{0:T(1024)(128)(4,1)}), s8[4194304]{0:T(1024)(128)(4,1)S(1)}, s32[]{:S(2)}) async-start(s8[12582912]{0:T(1024)(128)(4,1)} %bitcast.169), calls=%async_computation.17 | async-start | bytes 8388608
  251.6 2.0 copy-start.3
  253.7 3.1 copy-start.24
  257.2 2.0 copy-start.5
  259.2 3.3 copy-start.31
  259.2 5.5 slice-start.3
  259.2 5.6 slice-start.4
  262.5 2.5 slice-start.5
  264.5 7.1 %copy-start.14 = (bf16[768,16]{0,1:T(8,128)(2,1)}, bf16[768,16]{0,1:T(8,128)(2,1)S(1)}, u32[]{:S(2)}) copy-start(bf16[768,16]{0,1:T(8,128)(2,1)S(1)} %convolution_convert_fusion.3) | copy-start | bytes 73732
  265.0 11.1 %copy-start.16 = (bf16[768,16]{0,1:T(8,128)(2,1)}, bf16[768,16]{0,1:T(8,128)(2,1)S(1)}, u32[]{:S(2)}) copy-start(bf16[768,16]{0,1:T(8,128)(2,1)S(1)} %convolution_convert_fusion.2) | copy-start | bytes 73732
  280.4 6.4 %copy-start.9 = (bf16[1,16,4096]{2,1,0:T(8,128)(2,1)S(1)}, bf16[1,16,4096]{2,1,0:T(8,128)(2,1)}, u32[]{:S(2)}) copy-start(bf16[1,16,4096]{2,1,0:T(8,128)(2,1)} %param.22) | copy-start | bytes 393220
  286.8 167.1 %reduce-scatter.7.cloned.1.call-start = ((), (), s32[]{:S(2)}) async-start(), calls=%async_computation.7 | async-start | bytes 6684672
  299.1 238.5 %reduce-scatter.9.cloned.1.call-start = ((), (), s32[]{:S(2)}) async-start(), calls=%async_computation.8 | async-start | bytes 6684672
  299.2 8.9 %copy-start.6 = (bf16[1,448,4096]{2,1,0:T(8,128)(2,1)S(1)}, bf16[1,448,4096]{2,1,0:T(8,128)(2,1)}, u32[]{:S(2)}) copy-start(bf16[1,448,4096]{2,1,0:T(8,128)(2,1)} %param.18) | copy-start | bytes 11010052
  308.1 6.4 %copy-start.15 = (bf16[768,16]{0,1:T(8,128)(2,1)S(1)}, bf16[768,16]{0,1:T(8,128)(2,1)}, u32[]{:S(2)}) copy-start(bf16[768,16]{0,1:T(8,128)(2,1)} %copy-done.14) | copy-start | bytes 73732
  308.1 6.4 %copy-start.17 = (bf16[768,16]{0,1:T(8,128)(2,1)S(1)}, bf16[768,16]{0,1:T(8,128)(2,1)}, u32[]{:S(2)}) copy-start(bf16[768,16]{0,1:T(8,128)(2,1)} %copy-done.16) | copy-start | bytes 73732
  326.6 0.7 copy-start.33
  326.6 0.9 copy-start.36
  326.6 2.2 copy-start.23
  326.6 3.6 copy-start.27
  326.7 5.6 copy-start.30
  326.7 5.9 %copy-start.32 = (bf16[768,16]{0,1:T(8,128)(2,1)S(1)}, bf16[768,16]{0,1:T(8,128)(2,1)}, u32[]{:S(2)}) copy-start(bf16[768,16]{0,1:T(8,128)(2,1)} %copy-done.31) | copy-start | bytes 73732
  326.7 6.9 %copy-start.21 = (bf16[768,16]{0,1:T(8,128)(2,1)S(1)}, bf16[768,16]{0,1:T(8,128)(2,1)}, u32[]{:S(2)}) copy-start(bf16[768,16]{0,1:T(8,128)(2,1)} %copy-done.20) | copy-start | bytes 73732
  326.7 7.2 %copy-start.25 = (bf16[768,16]{0,1:T(8,128)(2,1)S(1)}, bf16[768,16]{0,1:T(8,128)(2,1)}, u32[]{:S(2)}) copy-start(bf16[768,16]{0,1:T(8,128)(2,1)} %copy-done.24) | copy-start | bytes 73732
  539.9 18.5 %all-to-all-start.1 = ((bf16[96,8,512]{2,0,1:T(8,128)(2,1)}), bf16[96,8,512]{2,0,1:T(8,128)(2,1)S(1)}, u32[]{:S(2)}, u32[]{:S(2)}) async-start(bf16[96,8,512]{2,0,1:T(8,128)(2,1)} %pad_maximum_fusion.1), calls=%async_computation.1 | async-start | bytes 1572864 | tf_op jit(solution)/shard_map/all_to_all | solution.py:178
  558.4 3.1 copy-start.1
Sparse Core Ops, SparseCore 0:
  58.9 89.7 all-gather.2
  150.9 89.5 all-gather.4
  286.9 82.4 all-reduce.6
  372.7 81.1 reduce-scatter.6
  457.2 80.4 reduce-scatter.8
where the time goes:
time: 576 us; the launch traced here: 568 us
  waiting for transfers between devices  324 us (56%)
  matrix products  136 us (24%)
  blocking collectives  45.7 us (8%)
  local copies, waits for them, and re-layouts  33 us (6%)
  between operations  15.6 us (3%)
  other arithmetic  6.67 us (1%)
  starting transfers between devices  6.65 us (1%)
    unnamed x8, waiting for transfers between devices  182 us
    dot_general x40, matrix products, contract_pair(): lax.dot_general(left, right, (((left_axis,), (right_axis,)), ((), ())), p...  136 us
    all_gather x2, waiting for transfers between devices, local(): gathered = lax.all_gather(part, 'dp', axis=0, tiled=True)  131 us
    all_to_all x1, blocking collectives, local(): lax.all_to_all(send_both, 'expert', split_axis=0, concat_axis=2, tiled=True)  27.4 us
    all_gather x1, blocking collectives, local(): lax.all_gather(lora_part, 'dp', axis=0, tiled=True).astype(jnp.float32)  18.3 us
  transfers between devices with their start and end apart: 6, of which 6 were waited for; matrix products, arithmetic and copies ran while one was open for 17% of the time, Pallas kernels for 0%

commit v1 on v0

--- a/solution.py
+++ b/solution.py
@@ -5,6 +5,16 @@
 
 ADAPTER_SCALE = 2.0
 NUM_CHUNKS = 2
+
+
+def gather_by_hops(x, axis, dim):
+    n_dev = lax.axis_size(axis)
+    moving, shards = (x, [x])
+    for _ in range(n_dev - 1):
+        moving = lax.ppermute(moving, axis, [(i, (i + 1) % n_dev) for i in range(n_dev)])
+        shards.insert(0, moving)
+    row_of_blocks = jnp.concatenate(shards, axis=dim)
+    return jnp.roll(row_of_blocks, (lax.axis_index(axis) + 1) * x.shape[dim], axis=dim)
 
 
 def contract_pair(left, right, left_axis, right_axis):
@@ -149,7 +159,7 @@
     owned_total = None
     for c in range(chunks):
         part = recv_both[c * piece : (c + 1) * piece]
-        gathered = lax.all_gather(part, "dp", axis=0, tiled=True)
+        gathered = gather_by_hops(part, "dp", 0)
         x_rows = gathered[:, :complete_width]
         dy_rows = gathered[:, complete_width:]
         rows_out, shared_slice, owned_slice = rows_backward_pass(x_rows, dy_rows, params)

time: 576 us -> 982 us (1.70)
  waiting for transfers between devices: 324 us -> 675 us
  local copies, waits for them, and re-layouts: 33 us -> 69.6 us
  other arithmetic: 6.67 us -> 32.6 us
  matrix products: 136 us -> 124 us
    ppermute x0 -> x30, waiting for transfers between devices: none -> 480 us  [gather_by_hops(): lax.ppermute(moving, axis, [(i, (i + 1) % n_dev) for i in range(n_dev)])]
    all_gather x2 -> x0, waiting for transfers between devices: 131 us -> none  [local(): gathered = lax.all_gather(part, 'dp', axis=0, tiled=True)]
    unnamed x99 -> x175, local copies, waits for them, and re-layouts: 9.66 us -> 43.3 us
    concatenate x0 -> x2, other arithmetic: none -> 26 us  [gather_by_hops(): jnp.roll(row_of_blocks, (lax.axis_index(axis) + 1) * x.shape[dim], axis=dim)]
    dot_general x40, matrix products: 136 us -> 124 us  [contract_pair(): lax.dot_general(left, right, (((left_axis,), (right_axis,)), ((), ())), p...]
    unnamed x8 -> x6, waiting for transfers between devices: 182 us -> 183 us
  transfers between devices with their start and end apart: 6 -> 34, of which waited for: 6 -> 33; matrix products, arithmetic and copies ran while one was open for 17% -> 8% of each run, Pallas kernels for 0% -> 0%
where the time goes in v1:
time: 982 us; the launch traced here: 973 us
  waiting for transfers between devices  675 us (69%)
  matrix products  124 us (13%)
  local copies, waits for them, and re-layouts  69.6 us (7%)
  blocking collectives  45.5 us (5%)
  other arithmetic  32.6 us (3%)
  between operations  15.8 us (2%)
    ppermute x30, waiting for transfers between devices, gather_by_hops(): lax.ppermute(moving, axis, [(i, (i + 1) % n_dev) for i in range(n_dev)])  480 us
    unnamed x6, waiting for transfers between devices  183 us
    dot_general x40, matrix products, contract_pair(): lax.dot_general(left, right, (((left_axis,), (right_axis,)), ((), ())), p...  124 us
    unnamed x175, local copies, waits for them, and re-layouts  43.3 us
    all_to_all x1, blocking collectives, local(): lax.all_to_all(send_both, 'expert', split_axis=0, concat_axis=2, tiled=True)  27.4 us
    concatenate x2, other arithmetic, gather_by_hops(): jnp.roll(row_of_blocks, (lax.axis_index(axis) + 1) * x.shape[dim], axis=dim)  26 us
  transfers between devices with their start and end apart: 34, of which 33 were waited for; matrix products, arithmetic and copies ran while one was open for 8% of the time, Pallas kernels for 0%

profile of v1, /device:TPU:1, one launch (start us, length us, event | category | flops | bytes accessed | tf_op | source)
XLA Modules:
  0.0 972.6 jit_solution(7104543738540236675)
XLA Ops:
  14.6 5.0 gather_fusion.1
  21.5 2.7 gather_fusion.2
  24.2 2.7 gather_fusion
  27.3 27.4 %all_to_all.20 = bf16[8,96,1024]{2,1,0:T(8,128)(2,1)S(1)} all-to-all(bf16[8,96,1024]{2,1,0:T(8,128)(2,1)S(1)} %pad_maximum_fusion), channel_id=1, replica_groups=mesh['dp'=16,'expert'=8] {'expert'}, dimensions={0} | all-to-all | bytes 3145728 | tf_op jit(solution)/shard_map/all_to_all | solution.py:154
  55.9 1.7 copy.71
  63.0 18.4 %collective-permute-done = bf16[48,8192]{1,0:T(8,128)(2,1)S(1)} collective-permute-done((bf16[48,8192]{1,0:T(8,128)(2,1)S(1)}, bf16[48,8192]{1,0:T(8,128)(2,1)S(1)}, u32[]{:S(2)}, u32[]{:S(2)}) %collective-permute-start) | collective-permute-done | bytes 786464 | tf_op jit(solution)/shard_map/ppermute | solution.py:14
  81.4 16.8 %collective-permute-done.15 = bf16[48,8192]{1,0:T(8,128)(2,1)S(1)} collective-permute-done((bf16[48,8192]{1,0:T(8,128)(2,1)S(1)}, bf16[48,8192]{1,0:T(8,128)(2,1)S(1)}, u32[]{:S(2)}, u32[]{:S(2)}) %collective-permute-start.15) | collective-permute-done | bytes 786464 | tf_op jit(solution)/shard_map/ppermute | solution.py:14
  98.2 16.8 %collective-permute-done.1 = bf16[48,8192]{1,0:T(8,128)(2,1)S(1)} collective-permute-done((bf16[48,8192]{1,0:T(8,128)(2,1)S(1)}, bf16[48,8192]{1,0:T(8,128)(2,1)S(1)}, u32[]{:S(2)}, u32[]{:S(2)}) %collective-permute-start.1) | collective-permute-done | bytes 786464 | tf_op jit(solution)/shard_map/ppermute | solution.py:14
  115.1 16.8 %collective-permute-done.16 = bf16[48,8192]{1,0:T(8,128)(2,1)S(1)} collective-permute-done((bf16[48,8192]{1,0:T(8,128)(2,1)S(1)}, bf16[48,8192]{1,0:T(8,128)(2,1)S(1)}, u32[]{:S(2)}, u32[]{:S(2)}) %collective-permute-start.16) | collective-permute-done | bytes 786464 | tf_op jit(solution)/shard_map/ppermute | solution.py:14
  131.9 16.8 %collective-permute-done.2 = bf16[48,8192]{1,0:T(8,128)(2,1)S(1)} collective-permute-done((bf16[48,8192]{1,0:T(8,128)(2,1)S(1)}, bf16[48,8192]{1,0:T(8,128)(2,1)S(1)}, u32[]{:S(2)}, u32[]{:S(2)}) %collective-permute-start.2) | collective-permute-done | bytes 786464 | tf_op jit(solution)/shard_map/ppermute | solution.py:14
  149.3 16.4 %collective-permute-done.17 = bf16[48,8192]{1,0:T(8,128)(2,1)S(1)} collective-permute-done((bf16[48,8192]{1,0:T(8,128)(2,1)S(1)}, bf16[48,8192]{1,0:T(8,128)(2,1)S(1)}, u32[]{:S(2)}, u32[]{:S(2)}) %collective-permute-start.17) | collective-permute-done | bytes 786464 | tf_op jit(solution)/shard_map/ppermute | solution.py:14
  166.5 16.0 %collective-permute-done.3 = bf16[48,8192]{1,0:T(8,128)(2,1)S(1)} collective-permute-done((bf16[48,8192]{1,0:T(8,128)(2,1)S(1)}, bf16[48,8192]{1,0:T(8,128)(2,1)S(1)}, u32[]{:S(2)}, u32[]{:S(2)}) %collective-permute-start.3) | collective-permute-done | bytes 786464 | tf_op jit(solution)/shard_map/ppermute | solution.py:14
  182.5 16.8 %collective-permute-done.18 = bf16[48,8192]{1,0:T(8,128)(2,1)S(1)} collective-permute-done((bf16[48,8192]{1,0:T(8,128)(2,1)S(1)}, bf16[48,8192]{1,0:T(8,128)(2,1)S(1)}, u32[]{:S(2)}, u32[]{:S(2)}) %collective-permute-start.18) | collective-permute-done | bytes 786464 | tf_op jit(solution)/shard_map/ppermute | solution.py:14
  200.3 16.0 %collective-permute-done.4 = bf16[48,8192]{1,0:T(8,128)(2,1)S(1)} collective-permute-done((bf16[48,8192]{1,0:T(8,128)(2,1)S(1)}, bf16[48,8192]{1,0:T(8,128)(2,1)S(1)}, u32[]{:S(2)}, u32[]{:S(2)}) %collective-permute-start.4) | collective-permute-done | bytes 786464 | tf_op jit(solution)/shard_map/ppermute | solution.py:14
  216.2 16.8 %collective-permute-done.19 = bf16[48,8192]{1,0:T(8,128)(2,1)S(1)} collective-permute-done((bf16[48,8192]{1,0:T(8,128)(2,1)S(1)}, bf16[48,8192]{1,0:T(8,128)(2,1)S(1)}, u32[]{:S(2)}, u32[]{:S(2)}) %collective-permute-start.19) | collective-permute-done | bytes 786464 | tf_op jit(solution)/shard_map/ppermute | solution.py:14
  233.9 16.0 %collective-permute-done.5 = bf16[48,8192]{1,0:T(8,128)(2,1)S(1)} collective-permute-done((bf16[48,8192]{1,0:T(8,128)(2,1)S(1)}, bf16[48,8192]{1,0:T(8,128)(2,1)S(1)}, u32[]{:S(2)}, u32[]{:S(2)}) %collective-permute-start.5) | collective-permute-done | bytes 786464 | tf_op jit(solution)/shard_map/ppermute | solution.py:14
  249.9 16.8 %collective-permute-done.20 = bf16[48,8192]{1,0:T(8,128)(2,1)S(1)} collective-permute-done((bf16[48,8192]{1,0:T(8,128)(2,1)S(1)}, bf16[48,8192]{1,0:T(8,128)(2,1)S(1)}, u32[]{:S(2)}, u32[]{:S(2)}) %collective-permute-start.20) | collective-permute-done | bytes 786464 | tf_op jit(solution)/shard_map/ppermute | solution.py:14
  267.7 15.9 %collective-permute-done.6 = bf16[48,8192]{1,0:T(8,128)(2,1)S(1)} collective-permute-done((bf16[48,8192]{1,0:T(8,128)(2,1)S(1)}, bf16[48,8192]{1,0:T(8,128)(2,1)S(1)}, u32[]{:S(2)}, u32[]{:S(2)}) %collective-permute-start.6) | collective-permute-done | bytes 786464 | tf_op jit(solution)/shard_map/ppermute | solution.py:14
  283.6 16.8 %collective-permute-done.21 = bf16[48,8192]{1,0:T(8,128)(2,1)S(1)} collective-permute-done((bf16[48,8192]{1,0:T(8,128)(2,1)S(1)}, bf16[48,8192]{1,0:T(8,128)(2,1)S(1)}, u32[]{:S(2)}, u32[]{:S(2)}) %collective-permute-start.21) | collective-permute-done | bytes 786464 | tf_op jit(solution)/shard_map/ppermute | solution.py:14
  301.4 15.9 %collective-permute-done.7 = bf16[48,8192]{1,0:T(8,128)(2,1)S(1)} collective-permute-done((bf16[48,8192]{1,0:T(8,128)(2,1)S(1)}, bf16[48,8192]{1,0:T(8,128)(2,1)S(1)}, u32[]{:S(2)}, u32[]{:S(2)}) %collective-permute-start.7) | collective-permute-done | bytes 786464 | tf_op jit(solution)/shard_map/ppermute | solution.py:14
  317.3 16.8 %collective-permute-done.22 = bf16[48,8192]{1,0:T(8,128)(2,1)S(1)} collective-permute-done((bf16[48,8192]{1,0:T(8,128)(2,1)S(1)}, bf16[48,8192]{1,0:T(8,128)(2,1)S(1)}, u32[]{:S(2)}, u32[]{:S(2)}) %collective-permute-start.22) | collective-permute-done | bytes 786464 | tf_op jit(solution)/shard_map/ppermute | solution.py:14
  335.1 15.9 %collective-permute-done.8 = bf16[48,8192]{1,0:T(8,128)(2,1)S(1)} collective-permute-done((bf16[48,8192]{1,0:T(8,128)(2,1)S(1)}, bf16[48,8192]{1,0:T(8,128)(2,1)S(1)}, u32[]{:S(2)}, u32[]{:S(2)}) %collective-permute-start.8) | collective-permute-done | bytes 786464 | tf_op jit(solution)/shard_map/ppermute | solution.py:14
  351.0 16.8 %collective-permute-done.23 = bf16[48,8192]{1,0:T(8,128)(2,1)S(1)} collective-permute-done((bf16[48,8192]{1,0:T(8,128)(2,1)S(1)}, bf16[48,8192]{1,0:T(8,128)(2,1)S(1)}, u32[]{:S(2)}, u32[]{:S(2)}) %collective-permute-start.23) | collective-permute-done | bytes 786464 | tf_op jit(solution)/shard_map/ppermute | solution.py:14
  368.8 15.9 %collective-permute-done.9 = bf16[48,8192]{1,0:T(8,128)(2,1)S(1)} collective-permute-done((bf16[48,8192]{1,0:T(8,128)(2,1)S(1)}, bf16[48,8192]{1,0:T(8,128)(2,1)S(1)}, u32[]{:S(2)}, u32[]{:S(2)}) %collective-permute-start.9) | collective-permute-done | bytes 786464 | tf_op jit(solution)/shard_map/ppermute | solution.py:14
  384.7 16.8 %collective-permute-done.24 = bf16[48,8192]{1,0:T(8,128)(2,1)S(1)} collective-permute-done((bf16[48,8192]{1,0:T(8,128)(2,1)S(1)}, bf16[48,8192]{1,0:T(8,128)(2,1)S(1)}, u32[]{:S(2)}, u32[]{:S(2)}) %collective-permute-start.24) | collective-permute-done | bytes 786464 | tf_op jit(solution)/shard_map/ppermute | solution.py:14
  402.5 16.0 %collective-permute-done.10 = bf16[48,8192]{1,0:T(8,128)(2,1)S(1)} collective-permute-done((bf16[48,8192]{1,0:T(8,128)(2,1)S(1)}, bf16[48,8192]{1,0:T(8,128)(2,1)S(1)}, u32[]{:S(2)}, u32[]{:S(2)}) %collective-permute-start.10) | collective-permute-done | bytes 786464 | tf_op jit(solution)/shard_map/ppermute | solution.py:14
  418.5 16.8 %collective-permute-done.25 = bf16[48,8192]{1,0:T(8,128)(2,1)S(1)} collective-permute-done((bf16[48,8192]{1,0:T(8,128)(2,1)S(1)}, bf16[48,8192]{1,0:T(8,128)(2,1)S(1)}, u32[]{:S(2)}, u32[]{:S(2)}) %collective-permute-start.25) | collective-permute-done | bytes 786464 | tf_op jit(solution)/shard_map/ppermute | solution.py:14
  436.2 15.9 %collective-permute-done.11 = bf16[48,8192]{1,0:T(8,128)(2,1)S(1)} collective-permute-done((bf16[48,8192]{1,0:T(8,128)(2,1)S(1)}, bf16[48,8192]{1,0:T(8,128)(2,1)S(1)}, u32[]{:S(2)}, u32[]{:S(2)}) %collective-permute-start.11) | collective-permute-done | bytes 786464 | tf_op jit(solution)/shard_map/ppermute | solution.py:14
  452.2 16.8 %collective-permute-done.26 = bf16[48,8192]{1,0:T(8,128)(2,1)S(1)} collective-permute-done((bf16[48,8192]{1,0:T(8,128)(2,1)S(1)}, bf16[48,8192]{1,0:T(8,128)(2,1)S(1)}, u32[]{:S(2)}, u32[]{:S(2)}) %collective-permute-start.26) | collective-permute-done | bytes 786464 | tf_op jit(solution)/shard_map/ppermute | solution.py:14
  469.9 16.0 %collective-permute-done.12 = bf16[48,8192]{1,0:T(8,128)(2,1)S(1)} collective-permute-done((bf16[48,8192]{1,0:T(8,128)(2,1)S(1)}, bf16[48,8192]{1,0:T(8,128)(2,1)S(1)}, u32[]{:S(2)}, u32[]{:S(2)}) %collective-permute-start.12) | collective-permute-done | bytes 786464 | tf_op jit(solution)/shard_map/ppermute | solution.py:14
  485.9 17.0 %collective-permute-done.27 = bf16[48,8192]{1,0:T(8,128)(2,1)} collective-permute-done((bf16[48,8192]{1,0:T(8,128)(2,1)S(1)}, bf16[48,8192]{1,0:T(8,128)(2,1)}, u32[]{:S(2)}, u32[]{:S(2)}) %collective-permute-start.27) | collective-permute-done | bytes 786464 | tf_op jit(solution)/shard_map/ppermute | solution.py:14
  502.8 16.8 %collective-permute-done.13 = bf16[48,8192]{1,0:T(8,128)(2,1)} collective-permute-done((bf16[48,8192]{1,0:T(8,128)(2,1)S(1)}, bf16[48,8192]{1,0:T(8,128)(2,1)}, u32[]{:S(2)}, u32[]{:S(2)}) %collective-permute-start.13) | collective-permute-done | bytes 786464 | tf_op jit(solution)/shard_map/ppermute | solution.py:14
  519.8 16.7 %collective-permute-done.28 = bf16[48,8192]{1,0:T(8,128)(2,1)} collective-permute-done((bf16[48,8192]{1,0:T(8,128)(2,1)}, bf16[48,8192]{1,0:T(8,128)(2,1)}, u32[]{:S(2)}, u32[]{:S(2)}) %collective-permute-start.28) | collective-permute-done | bytes 786464 | tf_op jit(solution)/shard_map/ppermute | solution.py:14
  536.7 16.7 %collective-permute-done.14 = bf16[48,8192]{1,0:T(8,128)(2,1)} collective-permute-done((bf16[48,8192]{1,0:T(8,128)(2,1)}, bf16[48,8192]{1,0:T(8,128)(2,1)}, u32[]{:S(2)}, u32[]{:S(2)}) %collective-permute-start.14) | collective-permute-done | bytes 786464 | tf_op jit(solution)/shard_map/ppermute | solution.py:14
  563.5 12.8 %fusion.1 = bf16[768,8192]{1,0:T(8,128)(2,1)S(1)} fusion(s32[]{:T(128)S(6)} %select_n.43, bf16[768,8192]{1,0:T(8,128)(2,1)S(1)} %constant_dynamic-update-slice_fusion), kind=kLoop, calls=%fused_computation.11 | loop fusion | flops 25165824 | bytes 25165828 | tf_op jit(solution)/shard_map/jit(_roll_dynamic)/concatenate | solution.py:17
  576.3 1.7 fusion.124
  580.8 4.5 constant_dynamic-update-slice_fusion.30
  585.2 2.1 constant_dynamic-update-slice_fusion.29
  599.7 13.2 %fusion = bf16[768,8192]{1,0:T(8,128)(2,1)S(1)} fusion(s32[]{:T(128)S(6)} %select_n.43, bf16[768,8192]{1,0:T(8,128)(2,1)} %constant_dynamic-update-slice_fusion.16), kind=kLoop, calls=%fused_computation.10 | loop fusion | flops 25165824 | bytes 25165828 | tf_op jit(solution)/shard_map/jit(_roll_dynamic)/concatenate | solution.py:17
  613.0 2.9 fusion.127
  619.4 1.7 fusion.118
  621.6 6.4 fusion.102
  628.5 4.2 fusion.92
  634.1 7.8 fusion.80
  642.1 6.3 fusion.31
  649.3 6.4 fusion.39
  656.1 3.1 fusion.107
  659.6 3.1 fusion.97
  663.0 4.5 fusion.71
  671.2 4.1 fusion.2
  675.3 4.6 fusion.25
  680.0 4.4 fusion.26
  684.3 4.7 fusion.22
  691.5 12.0 %add_convert_fusion.1 = bf16[768,4096]{1,0:T(8,128)(2,1)} fusion(f32[768,4096]{1,0:T(8,128)} %fusion.31, f32[768,4096]{1,0:T(8,128)} %fusion.39, bf16[16,4096]{1,0:T(8,128)(2,1)S(1)} %bitcast.258, bf16[16,4096]{1,0:T(8,128)(2,1)S(1)} %bitcast.256, bf16[16,768]{1,0:T(8,128)(2,1)S(1)} %bitcast.263, bf16[16,768]{1,0:T(8,128)(2,1)S(1)} %bitcast.262), kind=kOutput, calls=%fused_computation.13 | convolution fusion | flops 214532096 | bytes 31768576 | tf_op jit(solution)/shard_map/dot_general | solution.py:21
  703.6 8.6 fusion.27
  712.2 6.3 fusion.35
  718.5 12.1 %add_convert_fusion = bf16[768,4096]{1,0:T(8,128)(2,1)} fusion(f32[768,4096]{1,0:T(8,128)} %fusion.27, f32[768,4096]{1,0:T(8,128)} %fusion.35, bf16[16,4096]{1,0:T(8,128)(2,1)S(1)} %bitcast.259, bf16[16,4096]{1,0:T(8,128)(2,1)S(1)} %bitcast.257, bf16[16,768]{1,0:T(8,128)(2,1)S(1)} %bitcast.265, bf16[16,768]{1,0:T(8,128)(2,1)S(1)} %bitcast.264), kind=kOutput, calls=%fused_computation.12 | convolution fusion | flops 214532096 | bytes 31768576 | tf_op jit(solution)/shard_map/dot_general | solution.py:21
  733.6 2.1 fusion.131
  738.2 35.0 %all-reduce.7.cloned.1.call-done = bf16[128,1536]{1,0:T(8,128)(2,1)} async-done(((bf16[128,1536]{1,0:T(8,128)(2,1)}), bf16[128,1536]{1,0:T(8,128)(2,1)}) %all-reduce.7.cloned.1.call-update) | async-done | bytes 393232
  773.9 18.1 %all_gather.3 = bf16[128,1536]{1,0:T(8,128)(2,1)S(1)} all-gather(bf16[8,1536]{1,0:T(8,128)(2,1)S(1)} %constant_dynamic-slice_fusion), channel_id=1, replica_groups=mesh['dp'=16,'expert'=8] {'dp'}, dimensions={0}, use_global_device_ids=true | all-gather | bytes 417792 | tf_op jit(solution)/shard_map/all_gather | solution.py:183
  792.4 65.5 %reduce-scatter.7.cloned.1.call-done = bf16[1,48,4096]{2,1,0:T(8,128)(2,1)} async-done(((bf16[16,48,4096]{2,1,0:T(8,128)(2,1)}), bf16[1,48,4096]{2,1,0:T(8,128)(2,1)}) %reduce-scatter.7.cloned.1.call-update) | async-done | bytes 393232
  859.1 82.8 %reduce-scatter.9.cloned.1.call-done = bf16[1,48,4096]{2,1,0:T(8,128)(2,1)} async-done(((bf16[16,48,4096]{2,1,0:T(8,128)(2,1)}), bf16[1,48,4096]{2,1,0:T(8,128)(2,1)}) %reduce-scatter.9.cloned.1.call-update) | async-done | bytes 393232
  944.1 6.2 all-to-all-start.1
  951.2 11.4 %all-to-all-done.1 = bf16[96,8,512]{2,0,1:T(8,128)(2,1)S(1)} async-done(((bf16[96,8,512]{2,0,1:T(8,128)(2,1)}), bf16[96,8,512]{2,0,1:T(8,128)(2,1)S(1)}, u32[]{:S(2)}, u32[]{:S(2)}) %all-to-all-start.1) | async-done | bytes 786464 | tf_op jit(solution)/shard_map/all_to_all | solution.py:188
  (275 shorter events, 78.4 us)
Async XLA Ops:
  7.2 569.1 %copy-start = (bf16[1,4096,16]{1,2,0:T(8,128)(2,1)S(1)}, bf16[1,4096,16]{1,2,0:T(8,128)(2,1)}, u32[]{:S(2)}) copy-start(bf16[1,4096,16]{1,2,0:T(8,128)(2,1)} %param.27) | copy-start | bytes 393220
  7.2 765.9 %all-reduce.7.cloned.1.call-start = ((), (), s32[]{:S(2)}) async-start(), calls=%async_computation.4 | async-start | bytes 786432
  59.7 21.7 %collective-permute-start = (bf16[48,8192]{1,0:T(8,128)(2,1)S(1)}, bf16[48,8192]{1,0:T(8,128)(2,1)S(1)}, u32[]{:S(2)}, u32[]{:S(2)}) collective-permute-start(bf16[48,8192]{1,0:T(8,128)(2,1)S(1)} %bitcast.249), channel_id=1, source_target_pairs={{0,8},{8,16},{16,24},{24,32},{32,40},{40,48},{48,56},{56,64},{64,7... | collective-permute-start | bytes 2359304 | tf_op jit(solution)/shard_map/ppermute | solution.py:14
  61.6 36.6 %collective-permute-start.15 = (bf16[48,8192]{1,0:T(8,128)(2,1)S(1)}, bf16[48,8192]{1,0:T(8,128)(2,1)S(1)}, u32[]{:S(2)}, u32[]{:S(2)}) collective-permute-start(bf16[48,8192]{1,0:T(8,128)(2,1)S(1)} %bitcast.247), channel_id=1, source_target_pairs={{0,8},{8,16},{16,24},{24,32},{32,40},{40,48},{48,56},{56,64},{64,7... | collective-permute-start | bytes 2359304 | tf_op jit(solution)/shard_map/ppermute | solution.py:14
  81.4 118.0 %copy-start.9 = (bf16[48,8192]{1,0:T(8,128)(2,1)}, bf16[48,8192]{1,0:T(8,128)(2,1)S(1)}, u32[]{:S(2)}) copy-start(bf16[48,8192]{1,0:T(8,128)(2,1)S(1)} %collective-permute-done) | copy-start | bytes 2359300
  81.4 33.7 %collective-permute-start.1 = (bf16[48,8192]{1,0:T(8,128)(2,1)S(1)}, bf16[48,8192]{1,0:T(8,128)(2,1)S(1)}, u32[]{:S(2)}, u32[]{:S(2)}) collective-permute-start(bf16[48,8192]{1,0:T(8,128)(2,1)S(1)} %collective-permute-done), channel_id=1, source_target_pairs={{0,8},{8,16},{16,24},{24,32},{32,40},{40,48},{48,56},{56,64},{64,7... | collective-permute-start | bytes 2359304 | tf_op jit(solution)/shard_map/ppermute | solution.py:14
  98.2 33.7 %collective-permute-start.16 = (bf16[48,8192]{1,0:T(8,128)(2,1)S(1)}, bf16[48,8192]{1,0:T(8,128)(2,1)S(1)}, u32[]{:S(2)}, u32[]{:S(2)}) collective-permute-start(bf16[48,8192]{1,0:T(8,128)(2,1)S(1)} %collective-permute-done.15), channel_id=1, source_target_pairs={{0,8},{8,16},{16,24},{24,32},{32,40},{40,48},{48,56},{56,64},{64,7... | collective-permute-start | bytes 2359304 | tf_op jit(solution)/shard_map/ppermute | solution.py:14
  115.1 34.2 %copy-start.13 = (bf16[48,8192]{1,0:T(8,128)(2,1)}, bf16[48,8192]{1,0:T(8,128)(2,1)S(1)}, u32[]{:S(2)}) copy-start(bf16[48,8192]{1,0:T(8,128)(2,1)S(1)} %collective-permute-done.1) | copy-start | bytes 2359300
  115.1 33.7 %collective-permute-start.2 = (bf16[48,8192]{1,0:T(8,128)(2,1)S(1)}, bf16[48,8192]{1,0:T(8,128)(2,1)S(1)}, u32[]{:S(2)}, u32[]{:S(2)}) collective-permute-start(bf16[48,8192]{1,0:T(8,128)(2,1)S(1)} %collective-permute-done.1), channel_id=1, source_target_pairs={{0,8},{8,16},{16,24},{24,32},{32,40},{40,48},{48,56},{56,64},{64,7... | collective-permute-start | bytes 2359304 | tf_op jit(solution)/shard_map/ppermute | solution.py:14
  131.9 33.7 %collective-permute-start.17 = (bf16[48,8192]{1,0:T(8,128)(2,1)S(1)}, bf16[48,8192]{1,0:T(8,128)(2,1)S(1)}, u32[]{:S(2)}, u32[]{:S(2)}) collective-permute-start(bf16[48,8192]{1,0:T(8,128)(2,1)S(1)} %collective-permute-done.16), channel_id=1, source_target_pairs={{0,8},{8,16},{16,24},{24,32},{32,40},{40,48},{48,56},{56,64},{64,7... | collective-permute-start | bytes 2359304 | tf_op jit(solution)/shard_map/ppermute | solution.py:14
  148.8 118.0 %copy-start.17 = (bf16[48,8192]{1,0:T(8,128)(2,1)}, bf16[48,8192]{1,0:T(8,128)(2,1)S(1)}, u32[]{:S(2)}) copy-start(bf16[48,8192]{1,0:T(8,128)(2,1)S(1)} %collective-permute-done.2) | copy-start | bytes 2359300
  148.8 33.7 %collective-permute-start.3 = (bf16[48,8192]{1,0:T(8,128)(2,1)S(1)}, bf16[48,8192]{1,0:T(8,128)(2,1)S(1)}, u32[]{:S(2)}, u32[]{:S(2)}) collective-permute-start(bf16[48,8192]{1,0:T(8,128)(2,1)S(1)} %collective-permute-done.2), channel_id=1, source_target_pairs={{0,8},{8,16},{16,24},{24,32},{32,40},{40,48},{48,56},{56,64},{64,7... | collective-permute-start | bytes 2359304 | tf_op jit(solution)/shard_map/ppermute | solution.py:14
  166.5 32.8 %collective-permute-start.18 = (bf16[48,8192]{1,0:T(8,128)(2,1)S(1)}, bf16[48,8192]{1,0:T(8,128)(2,1)S(1)}, u32[]{:S(2)}, u32[]{:S(2)}) collective-permute-start(bf16[48,8192]{1,0:T(8,128)(2,1)S(1)} %collective-permute-done.17), channel_id=1, source_target_pairs={{0,8},{8,16},{16,24},{24,32},{32,40},{40,48},{48,56},{56,64},{64,7... | collective-permute-start | bytes 2359304 | tf_op jit(solution)/shard_map/ppermute | solution.py:14
  182.5 118.0 %copy-start.21 = (bf16[48,8192]{1,0:T(8,128)(2,1)}, bf16[48,8192]{1,0:T(8,128)(2,1)S(1)}, u32[]{:S(2)}) copy-start(bf16[48,8192]{1,0:T(8,128)(2,1)S(1)} %collective-permute-done.3) | copy-start | bytes 2359300
  182.5 33.7 %collective-permute-start.4 = (bf16[48,8192]{1,0:T(8,128)(2,1)S(1)}, bf16[48,8192]{1,0:T(8,128)(2,1)S(1)}, u32[]{:S(2)}, u32[]{:S(2)}) collective-permute-start(bf16[48,8192]{1,0:T(8,128)(2,1)S(1)} %collective-permute-done.3), channel_id=1, source_target_pairs={{0,8},{8,16},{16,24},{24,32},{32,40},{40,48},{48,56},{56,64},{64,7... | collective-permute-start | bytes 2359304 | tf_op jit(solution)/shard_map/ppermute | solution.py:14
  199.4 33.7 %collective-permute-start.19 = (bf16[48,8192]{1,0:T(8,128)(2,1)S(1)}, bf16[48,8192]{1,0:T(8,128)(2,1)S(1)}, u32[]{:S(2)}, u32[]{:S(2)}) collective-permute-start(bf16[48,8192]{1,0:T(8,128)(2,1)S(1)} %collective-permute-done.18), channel_id=1, source_target_pairs={{0,8},{8,16},{16,24},{24,32},{32,40},{40,48},{48,56},{56,64},{64,7... | collective-permute-start | bytes 2359304 | tf_op jit(solution)/shard_map/ppermute | solution.py:14
  216.2 118.0 %copy-start.25 = (bf16[48,8192]{1,0:T(8,128)(2,1)}, bf16[48,8192]{1,0:T(8,128)(2,1)S(1)}, u32[]{:S(2)}) copy-start(bf16[48,8192]{1,0:T(8,128)(2,1)S(1)} %collective-permute-done.4) | copy-start | bytes 2359300
  216.2 33.7 %collective-permute-start.5 = (bf16[48,8192]{1,0:T(8,128)(2,1)S(1)}, bf16[48,8192]{1,0:T(8,128)(2,1)S(1)}, u32[]{:S(2)}, u32[]{:S(2)}) collective-permute-start(bf16[48,8192]{1,0:T(8,128)(2,1)S(1)} %collective-permute-done.4), channel_id=1, source_target_pairs={{0,8},{8,16},{16,24},{24,32},{32,40},{40,48},{48,56},{56,64},{64,7... | collective-permute-start | bytes 2359304 | tf_op jit(solution)/shard_map/ppermute | solution.py:14
  233.9 32.8 %collective-permute-start.20 = (bf16[48,8192]{1,0:T(8,128)(2,1)S(1)}, bf16[48,8192]{1,0:T(8,128)(2,1)S(1)}, u32[]{:S(2)}, u32[]{:S(2)}) collective-permute-start(bf16[48,8192]{1,0:T(8,128)(2,1)S(1)} %collective-permute-done.19), channel_id=1, source_target_pairs={{0,8},{8,16},{16,24},{24,32},{32,40},{40,48},{48,56},{56,64},{64,7... | collective-permute-start | bytes 2359304 | tf_op jit(solution)/shard_map/ppermute | solution.py:14
  249.9 118.0 %copy-start.29 = (bf16[48,8192]{1,0:T(8,128)(2,1)}, bf16[48,8192]{1,0:T(8,128)(2,1)S(1)}, u32[]{:S(2)}) copy-start(bf16[48,8192]{1,0:T(8,128)(2,1)S(1)} %collective-permute-done.5) | copy-start | bytes 2359300
  249.9 33.7 %collective-permute-start.6 = (bf16[48,8192]{1,0:T(8,128)(2,1)S(1)}, bf16[48,8192]{1,0:T(8,128)(2,1)S(1)}, u32[]{:S(2)}, u32[]{:S(2)}) collective-permute-start(bf16[48,8192]{1,0:T(8,128)(2,1)S(1)} %collective-permute-done.5), channel_id=1, source_target_pairs={{0,8},{8,16},{16,24},{24,32},{32,40},{40,48},{48,56},{56,64},{64,7... | collective-permute-start | bytes 2359304 | tf_op jit(solution)/shard_map/ppermute | solution.py:14
  266.8 33.7 %collective-permute-start.21 = (bf16[48,8192]{1,0:T(8,128)(2,1)S(1)}, bf16[48,8192]{1,0:T(8,128)(2,1)S(1)}, u32[]{:S(2)}, u32[]{:S(2)}) collective-permute-start(bf16[48,8192]{1,0:T(8,128)(2,1)S(1)} %collective-permute-done.20), channel_id=1, source_target_pairs={{0,8},{8,16},{16,24},{24,32},{32,40},{40,48},{48,56},{56,64},{64,7... | collective-permute-start | bytes 2359304 | tf_op jit(solution)/shard_map/ppermute | solution.py:14
  283.6 118.0 %copy-start.33 = (bf16[48,8192]{1,0:T(8,128)(2,1)}, bf16[48,8192]{1,0:T(8,128)(2,1)S(1)}, u32[]{:S(2)}) copy-start(bf16[48,8192]{1,0:T(8,128)(2,1)S(1)} %collective-permute-done.6) | copy-start | bytes 2359300
  283.6 33.7 %collective-permute-start.7 = (bf16[48,8192]{1,0:T(8,128)(2,1)S(1)}, bf16[48,8192]{1,0:T(8,128)(2,1)S(1)}, u32[]{:S(2)}, u32[]{:S(2)}) collective-permute-start(bf16[48,8192]{1,0:T(8,128)(2,1)S(1)} %collective-permute-done.6), channel_id=1, source_target_pairs={{0,8},{8,16},{16,24},{24,32},{32,40},{40,48},{48,56},{56,64},{64,7... | collective-permute-start | bytes 2359304 | tf_op jit(solution)/shard_map/ppermute | solution.py:14
  300.5 33.7 %collective-permute-start.22 = (bf16[48,8192]{1,0:T(8,128)(2,1)S(1)}, bf16[48,8192]{1,0:T(8,128)(2,1)S(1)}, u32[]{:S(2)}, u32[]{:S(2)}) collective-permute-start(bf16[48,8192]{1,0:T(8,128)(2,1)S(1)} %collective-permute-done.21), channel_id=1, source_target_pairs={{0,8},{8,16},{16,24},{24,32},{32,40},{40,48},{48,56},{56,64},{64,7... | collective-permute-start | bytes 2359304 | tf_op jit(solution)/shard_map/ppermute | solution.py:14
  317.3 118.0 %copy-start.37 = (bf16[48,8192]{1,0:T(8,128)(2,1)}, bf16[48,8192]{1,0:T(8,128)(2,1)S(1)}, u32[]{:S(2)}) copy-start(bf16[48,8192]{1,0:T(8,128)(2,1)S(1)} %collective-permute-done.7) | copy-start | bytes 2359300
  317.3 33.7 %collective-permute-start.8 = (bf16[48,8192]{1,0:T(8,128)(2,1)S(1)}, bf16[48,8192]{1,0:T(8,128)(2,1)S(1)}, u32[]{:S(2)}, u32[]{:S(2)}) collective-permute-start(bf16[48,8192]{1,0:T(8,128)(2,1)S(1)} %collective-permute-done.7), channel_id=1, source_target_pairs={{0,8},{8,16},{16,24},{24,32},{32,40},{40,48},{48,56},{56,64},{64,7... | collective-permute-start | bytes 2359304 | tf_op jit(solution)/shard_map/ppermute | solution.py:14
  334.2 33.7 %collective-permute-start.23 = (bf16[48,8192]{1,0:T(8,128)(2,1)S(1)}, bf16[48,8192]{1,0:T(8,128)(2,1)S(1)}, u32[]{:S(2)}, u32[]{:S(2)}) collective-permute-start(bf16[48,8192]{1,0:T(8,128)(2,1)S(1)} %collective-permute-done.22), channel_id=1, source_target_pairs={{0,8},{8,16},{16,24},{24,32},{32,40},{40,48},{48,56},{56,64},{64,7... | collective-permute-start | bytes 2359304 | tf_op jit(solution)/shard_map/ppermute | solution.py:14
  351.0 118.0 %copy-start.40 = (bf16[48,8192]{1,0:T(8,128)(2,1)}, bf16[48,8192]{1,0:T(8,128)(2,1)S(1)}, u32[]{:S(2)}) copy-start(bf16[48,8192]{1,0:T(8,128)(2,1)S(1)} %collective-permute-done.8) | copy-start | bytes 2359300
  351.0 33.7 %collective-permute-start.9 = (bf16[48,8192]{1,0:T(8,128)(2,1)S(1)}, bf16[48,8192]{1,0:T(8,128)(2,1)S(1)}, u32[]{:S(2)}, u32[]{:S(2)}) collective-permute-start(bf16[48,8192]{1,0:T(8,128)(2,1)S(1)} %collective-permute-done.8), channel_id=1, source_target_pairs={{0,8},{8,16},{16,24},{24,32},{32,40},{40,48},{48,56},{56,64},{64,7... | collective-permute-start | bytes 2359304 | tf_op jit(solution)/shard_map/ppermute | solution.py:14
  367.9 33.7 %collective-permute-start.24 = (bf16[48,8192]{1,0:T(8,128)(2,1)S(1)}, bf16[48,8192]{1,0:T(8,128)(2,1)S(1)}, u32[]{:S(2)}, u32[]{:S(2)}) collective-permute-start(bf16[48,8192]{1,0:T(8,128)(2,1)S(1)} %collective-permute-done.23), channel_id=1, source_target_pairs={{0,8},{8,16},{16,24},{24,32},{32,40},{40,48},{48,56},{56,64},{64,7... | collective-permute-start | bytes 2359304 | tf_op jit(solution)/shard_map/ppermute | solution.py:14
  384.7 118.1 %copy-start.43 = (bf16[48,8192]{1,0:T(8,128)(2,1)}, bf16[48,8192]{1,0:T(8,128)(2,1)S(1)}, u32[]{:S(2)}) copy-start(bf16[48,8192]{1,0:T(8,128)(2,1)S(1)} %collective-permute-done.9) | copy-start | bytes 2359300
  384.7 33.7 %collective-permute-start.10 = (bf16[48,8192]{1,0:T(8,128)(2,1)S(1)}, bf16[48,8192]{1,0:T(8,128)(2,1)S(1)}, u32[]{:S(2)}, u32[]{:S(2)}) collective-permute-start(bf16[48,8192]{1,0:T(8,128)(2,1)S(1)} %collective-permute-done.9), channel_id=1, source_target_pairs={{0,8},{8,16},{16,24},{24,32},{32,40},{40,48},{48,56},{56,64},{64,7... | collective-permute-start | bytes 2359304 | tf_op jit(solution)/shard_map/ppermute | solution.py:14
  401.6 33.7 %collective-permute-start.25 = (bf16[48,8192]{1,0:T(8,128)(2,1)S(1)}, bf16[48,8192]{1,0:T(8,128)(2,1)S(1)}, u32[]{:S(2)}, u32[]{:S(2)}) collective-permute-start(bf16[48,8192]{1,0:T(8,128)(2,1)S(1)} %collective-permute-done.24), channel_id=1, source_target_pairs={{0,8},{8,16},{16,24},{24,32},{32,40},{40,48},{48,56},{56,64},{64,7... | collective-permute-start | bytes 2359304 | tf_op jit(solution)/shard_map/ppermute | solution.py:14
  418.4 84.4 %copy-start.44 = (bf16[48,8192]{1,0:T(8,128)(2,1)}, bf16[48,8192]{1,0:T(8,128)(2,1)S(1)}, u32[]{:S(2)}) copy-start(bf16[48,8192]{1,0:T(8,128)(2,1)S(1)} %collective-permute-done.10) | copy-start | bytes 2359300
  418.4 33.7 %collective-permute-start.11 = (bf16[48,8192]{1,0:T(8,128)(2,1)S(1)}, bf16[48,8192]{1,0:T(8,128)(2,1)S(1)}, u32[]{:S(2)}, u32[]{:S(2)}) collective-permute-start(bf16[48,8192]{1,0:T(8,128)(2,1)S(1)} %collective-permute-done.10), channel_id=1, source_target_pairs={{0,8},{8,16},{16,24},{24,32},{32,40},{40,48},{48,56},{56,64},{64,7... | collective-permute-start | bytes 2359304 | tf_op jit(solution)/shard_map/ppermute | solution.py:14
  435.3 33.7 %collective-permute-start.26 = (bf16[48,8192]{1,0:T(8,128)(2,1)S(1)}, bf16[48,8192]{1,0:T(8,128)(2,1)S(1)}, u32[]{:S(2)}, u32[]{:S(2)}) collective-permute-start(bf16[48,8192]{1,0:T(8,128)(2,1)S(1)} %collective-permute-done.25), channel_id=1, source_target_pairs={{0,8},{8,16},{16,24},{24,32},{32,40},{40,48},{48,56},{56,64},{64,7... | collective-permute-start | bytes 2359304 | tf_op jit(solution)/shard_map/ppermute | solution.py:14
  452.2 67.5 %copy-start.45 = (bf16[48,8192]{1,0:T(8,128)(2,1)}, bf16[48,8192]{1,0:T(8,128)(2,1)S(1)}, u32[]{:S(2)}) copy-start(bf16[48,8192]{1,0:T(8,128)(2,1)S(1)} %collective-permute-done.11) | copy-start | bytes 2359300
  452.2 33.7 %collective-permute-start.12 = (bf16[48,8192]{1,0:T(8,128)(2,1)S(1)}, bf16[48,8192]{1,0:T(8,128)(2,1)S(1)}, u32[]{:S(2)}, u32[]{:S(2)}) collective-permute-start(bf16[48,8192]{1,0:T(8,128)(2,1)S(1)} %collective-permute-done.11), channel_id=1, source_target_pairs={{0,8},{8,16},{16,24},{24,32},{32,40},{40,48},{48,56},{56,64},{64,7... | collective-permute-start | bytes 2359304 | tf_op jit(solution)/shard_map/ppermute | solution.py:14
  469.0 33.8 %collective-permute-start.27 = (bf16[48,8192]{1,0:T(8,128)(2,1)S(1)}, bf16[48,8192]{1,0:T(8,128)(2,1)}, u32[]{:S(2)}, u32[]{:S(2)}) collective-permute-start(bf16[48,8192]{1,0:T(8,128)(2,1)S(1)} %collective-permute-done.26), channel_id=1, source_target_pairs={{0,8},{8,16},{16,24},{24,32},{32,40},{40,48},{48,56},{56,64},{64,7... | collective-permute-start | bytes 2359304 | tf_op jit(solution)/shard_map/ppermute | solution.py:14
  485.9 33.8 %copy-start.46 = (bf16[48,8192]{1,0:T(8,128)(2,1)}, bf16[48,8192]{1,0:T(8,128)(2,1)S(1)}, u32[]{:S(2)}) copy-start(bf16[48,8192]{1,0:T(8,128)(2,1)S(1)} %collective-permute-done.12) | copy-start | bytes 2359300
  485.9 33.8 %collective-permute-start.13 = (bf16[48,8192]{1,0:T(8,128)(2,1)S(1)}, bf16[48,8192]{1,0:T(8,128)(2,1)}, u32[]{:S(2)}, u32[]{:S(2)}) collective-permute-start(bf16[48,8192]{1,0:T(8,128)(2,1)S(1)} %collective-permute-done.12), channel_id=1, source_target_pairs={{0,8},{8,16},{16,24},{24,32},{32,40},{40,48},{48,56},{56,64},{64,7... | collective-permute-start | bytes 2359304 | tf_op jit(solution)/shard_map/ppermute | solution.py:14
  502.8 33.7 %collective-permute-start.28 = (bf16[48,8192]{1,0:T(8,128)(2,1)}, bf16[48,8192]{1,0:T(8,128)(2,1)}, u32[]{:S(2)}, u32[]{:S(2)}) collective-permute-start(bf16[48,8192]{1,0:T(8,128)(2,1)} %collective-permute-done.27), channel_id=1, source_target_pairs={{0,8},{8,16},{16,24},{24,32},{32,40},{40,48},{48,56},{56,64},{64,7... | collective-permute-start | bytes 2359304 | tf_op jit(solution)/shard_map/ppermute | solution.py:14
  519.7 33.7 %collective-permute-start.14 = (bf16[48,8192]{1,0:T(8,128)(2,1)}, bf16[48,8192]{1,0:T(8,128)(2,1)}, u32[]{:S(2)}, u32[]{:S(2)}) collective-permute-start(bf16[48,8192]{1,0:T(8,128)(2,1)} %collective-permute-done.13), channel_id=1, source_target_pairs={{0,8},{8,16},{16,24},{24,32},{32,40},{40,48},{48,56},{56,64},{64,7... | collective-permute-start | bytes 2359304 | tf_op jit(solution)/shard_map/ppermute | solution.py:14
  519.7 43.2 %copy-start.34 = (bf16[48,8192]{1,0:T(8,128)(2,1)S(1)}, bf16[48,8192]{1,0:T(8,128)(2,1)}, u32[]{:S(2)}) copy-start(bf16[48,8192]{1,0:T(8,128)(2,1)} %copy-done.33) | copy-start | bytes 2359300
  519.7 43.2 %copy-start.30 = (bf16[48,8192]{1,0:T(8,128)(2,1)S(1)}, bf16[48,8192]{1,0:T(8,128)(2,1)}, u32[]{:S(2)}) copy-start(bf16[48,8192]{1,0:T(8,128)(2,1)} %copy-done.29) | copy-start | bytes 2359300
  519.7 43.3 %copy-start.26 = (bf16[48,8192]{1,0:T(8,128)(2,1)S(1)}, bf16[48,8192]{1,0:T(8,128)(2,1)}, u32[]{:S(2)}) copy-start(bf16[48,8192]{1,0:T(8,128)(2,1)} %copy-done.25) | copy-start | bytes 2359300
  519.7 43.4 %copy-start.22 = (bf16[48,8192]{1,0:T(8,128)(2,1)S(1)}, bf16[48,8192]{1,0:T(8,128)(2,1)}, u32[]{:S(2)}) copy-start(bf16[48,8192]{1,0:T(8,128)(2,1)} %copy-done.21) | copy-start | bytes 2359300
  519.7 43.4 %copy-start.18 = (bf16[48,8192]{1,0:T(8,128)(2,1)S(1)}, bf16[48,8192]{1,0:T(8,128)(2,1)}, u32[]{:S(2)}) copy-start(bf16[48,8192]{1,0:T(8,128)(2,1)} %copy-done.17) | copy-start | bytes 2359300
  519.8 43.5 %copy-start.14 = (bf16[48,8192]{1,0:T(8,128)(2,1)S(1)}, bf16[48,8192]{1,0:T(8,128)(2,1)}, u32[]{:S(2)}) copy-start(bf16[48,8192]{1,0:T(8,128)(2,1)} %copy-done.13) | copy-start | bytes 2359300
  519.8 43.5 %copy-start.10 = (bf16[48,8192]{1,0:T(8,128)(2,1)S(1)}, bf16[48,8192]{1,0:T(8,128)(2,1)}, u32[]{:S(2)}) copy-start(bf16[48,8192]{1,0:T(8,128)(2,1)} %copy-done.9) | copy-start | bytes 2359300
  536.5 43.3 %collective-permute-start.29 = (bf16[48,8192]{1,0:T(8,128)(2,1)}, bf16[48,8192]{1,0:T(8,128)(2,1)S(1)}, u32[]{:S(2)}, u32[]{:S(2)}) collective-permute-start(bf16[48,8192]{1,0:T(8,128)(2,1)} %collective-permute-done.28), channel_id=1, source_target_pairs={{0,8},{8,16},{16,24},{24,32},{32,40},{40,48},{48,56},{56,64},{64,7... | collective-permute-start | bytes 2359304 | tf_op jit(solution)/shard_map/ppermute | solution.py:14
  576.2 57.9 %copy-start.2 = (bf16[768,8192]{1,0:T(8,128)(2,1)}, bf16[768,8192]{1,0:T(8,128)(2,1)S(1)}, u32[]{:S(2)}) copy-start(bf16[768,8192]{1,0:T(8,128)(2,1)S(1)} %fusion.1) | copy-start | bytes 37748740
  578.0 43.2 %copy-start.56 = (bf16[768,16]{0,1:T(8,128)(2,1)}, bf16[768,16]{0,1:T(8,128)(2,1)S(1)}, u32[]{:S(2)}) copy-start(bf16[768,16]{0,1:T(8,128)(2,1)S(1)} %fusion.124) | copy-start | bytes 73732
  579.8 48.2 %copy-start.54 = (bf16[768,16]{0,1:T(8,128)(2,1)}, bf16[768,16]{0,1:T(8,128)(2,1)S(1)}, u32[]{:S(2)}) copy-start(bf16[768,16]{0,1:T(8,128)(2,1)S(1)} %fusion.115) | copy-start | bytes 73732
  613.0 56.6 %copy-start.3 = (bf16[768,8192]{1,0:T(8,128)(2,1)}, bf16[768,8192]{1,0:T(8,128)(2,1)S(1)}, u32[]{:S(2)}) copy-start(bf16[768,8192]{1,0:T(8,128)(2,1)S(1)} %fusion) | copy-start | bytes 37748740
  617.7 41.5 %copy-start.58 = (bf16[768,16]{0,1:T(8,128)(2,1)}, bf16[768,16]{0,1:T(8,128)(2,1)S(1)}, u32[]{:S(2)}) copy-start(bf16[768,16]{0,1:T(8,128)(2,1)S(1)} %fusion.121) | copy-start | bytes 73732
  621.2 41.5 %copy-start.60 = (bf16[768,16]{0,1:T(8,128)(2,1)}, bf16[768,16]{0,1:T(8,128)(2,1)S(1)}, u32[]{:S(2)}) copy-start(bf16[768,16]{0,1:T(8,128)(2,1)S(1)} %fusion.118) | copy-start | bytes 73732
  691.4 166.5 %reduce-scatter.7.cloned.1.call-start = ((), (), s32[]{:S(2)}) async-start(), calls=%async_computation.5 | async-start | bytes 6684672
  703.5 238.4 %reduce-scatter.9.cloned.1.call-start = ((), (), s32[]{:S(2)}) async-start(), calls=%async_computation.6 | async-start | bytes 6684672
  718.5 18.4 %copy-start.55 = (bf16[768,16]{0,1:T(8,128)(2,1)S(1)}, bf16[768,16]{0,1:T(8,128)(2,1)}, u32[]{:S(2)}) copy-start(bf16[768,16]{0,1:T(8,128)(2,1)} %copy-done.54) | copy-start | bytes 73732
  718.5 18.7 %copy-start.59 = (bf16[768,16]{0,1:T(8,128)(2,1)S(1)}, bf16[768,16]{0,1:T(8,128)(2,1)}, u32[]{:S(2)}) copy-start(bf16[768,16]{0,1:T(8,128)(2,1)} %copy-done.58) | copy-start | bytes 73732
  730.6 235.0 %copy-start.1 = (bf16[1,4096,16]{1,2,0:T(8,128)(2,1)S(1)}, bf16[1,4096,16]{1,2,0:T(8,128)(2,1)}, u32[]{:S(2)}) copy-start(bf16[1,4096,16]{1,2,0:T(8,128)(2,1)} %param.27) | copy-start | bytes 393220
  944.1 18.5 %all-to-all-start.1 = ((bf16[96,8,512]{2,0,1:T(8,128)(2,1)}), bf16[96,8,512]{2,0,1:T(8,128)(2,1)S(1)}, u32[]{:S(2)}, u32[]{:S(2)}) async-start(bf16[96,8,512]{2,0,1:T(8,128)(2,1)} %pad_maximum_fusion.1), calls=%async_computation.1 | async-start | bytes 1572864 | tf_op jit(solution)/shard_map/all_to_all | solution.py:188
  (39 other events, 353.7 us)
Sparse Core Ops, SparseCore 0:
  691.5 81.5 all-reduce.6
  776.5 81.3 reduce-scatter.6
  861.3 80.5 reduce-scatter.8
